TPU v7x, 32 devices: a whole 2x2x4 slice. The times are simulated.
32 devices in a mesh: screen: 2 (over x), pool: 8 (over z, y), dap: 2 (over core).
Axes of the slice: x: 2, y: 2, z: 4, core: 2. Of those that a mesh axis runs over, the one named last changes fastest.
Arguments:
- pair_rep: bfloat16 [352, 16, 16, 128], P(('screen', 'pool'), 'dap'), parts along dimension 0, may hold values from -6 to 6
- alignment: bfloat16 [352, 16, 16, 256], P(('screen', 'pool'), None, 'dap'), parts along dimension 0, may hold values from -6 to 6
- lengths: int32 [352], P('screen'), parts along dimension 0, may hold values from 8 to 16, as said below
- chain_breaks: int32 [352], P('screen'), parts along dimension 0, may hold values from 1 to 15, as said below
- shifts: int32 [44], P('screen'), parts along dimension 0, may hold values from 0 to 7, as said below
- alignment_proj: bfloat16 [256, 64], replicated, may hold values from -0.375 to 0.375
- outer_proj: bfloat16 [1024, 128], replicated, may hold values from -0.75 to 0.75
- chain_bias: bfloat16 [2, 128], replicated, may hold values from -4 to 4
- outgoing_ab: bfloat16 [128, 512], replicated, may hold values from -0.5 to 0.5
- outgoing_gate: bfloat16 [128, 128], replicated, may hold values from -0.5 to 0.5
- outgoing_proj: bfloat16 [128, 128], replicated, may hold values from -0.5 to 0.5
- incoming_ab: bfloat16 [128, 512], replicated, may hold values from -0.5 to 0.5
- incoming_gate: bfloat16 [128, 128], replicated, may hold values from -0.5 to 0.5
- incoming_proj: bfloat16 [128, 128], replicated, may hold values from -0.5 to 0.5
Outputs:
- pair_out: bfloat16 [352, 16, 16, 128], P(('screen', 'pool'), 'dap'), parts along dimension 0
There are 2 independent parts, one for each index of `screen`. A program takes and returns all parts, laid end to end along the dimension named above; an argument that names none is the same for every part. Nothing has to cross between parts.
Inputs may be any that keep to these rules, and one draw needn't show every extreme that they name: The complex in slot s of group g goes to group (g + shifts[s]) mod 8 and keeps slot s. No value occurs more than 6 times in shifts, and one value occurs exactly 6 times. `lengths`: at least one complex has exactly 16 residues. The bait chain is residues 0 to chain_breaks - 1, the candidate chain the rest up to the complex's length.
All inputs are finite; a program needn't handle non-finite values.
Results may differ from a plain program's by a relative error of at most 0.0066.
Values may be sent and summed in bfloat16 or wider, within the bound.
No kernel may reach another device: no remote copies, remote signals or barrier semaphores. Data moves between devices by JAX's collectives and lax.ppermute only.
A program may use at most 128 MiB of HBM per device.

v0:
```python
import jax
import jax.numpy as jnp
from jax import lax
from jax.sharding import PartitionSpec as P

EPSILON = 1e-05


def layer_normalize(values):
    values = values.astype(jnp.float32)
    center = jnp.mean(values, axis=-1, keepdims=True)
    spread = jnp.mean(jnp.square(values - center), axis=-1, keepdims=True)
    return (values - center) * lax.rsqrt(spread + EPSILON)


def triangle(stream, pair_mask, weight_ab, weight_gate, weight_proj):
    normalized_rows = layer_normalize(stream).astype(jnp.bfloat16)
    project = jnp.dot(normalized_rows, weight_ab, preferred_element_type=jnp.float32)
    hidden_width = weight_proj.shape[0]
    left_side = (
        jax.nn.sigmoid(project[..., hidden_width : 2 * hidden_width]) * project[..., :hidden_width]
    )
    left_side = (left_side * pair_mask[..., None]).astype(jnp.bfloat16)
    right_side = (
        jax.nn.sigmoid(project[..., 3 * hidden_width :])
        * project[..., 2 * hidden_width : 3 * hidden_width]
    )
    right_side = (right_side * pair_mask[..., None]).astype(jnp.bfloat16)
    product = jnp.einsum(
        "sikc,sjkc->sijc",
        left_side,
        lax.all_gather(right_side, "dap", axis=1, tiled=True),
        preferred_element_type=jnp.float32,
    )
    normed_product = layer_normalize(product).astype(jnp.bfloat16)
    gating = jax.nn.sigmoid(
        jnp.dot(normalized_rows, weight_gate, preferred_element_type=jnp.float32)
    )
    return gating * jnp.dot(normed_product, weight_proj, preferred_element_type=jnp.float32)


def pair_update_portion(
    pairwise_block, alignment_block, local_lengths, local_chain_breaks, starting_row, weight_params
):
    (
        alignment_proj,
        outer_proj,
        chain_bias,
        outgoing_ab,
        outgoing_gate,
        outgoing_proj,
        incoming_ab,
        incoming_gate,
        incoming_proj,
    ) = weight_params
    half_rows = pairwise_block.shape[1]
    full_rows = pairwise_block.shape[2]
    places = jnp.arange(full_rows, dtype=jnp.int32)
    rows_here = starting_row + jnp.arange(half_rows, dtype=jnp.int32)
    mask_full = (places[None, :] < local_lengths[:, None]).astype(jnp.float32)
    mask_rows = (rows_here[None, :] < local_lengths[:, None]).astype(jnp.float32)
    pair_mask = mask_rows[:, :, None] * mask_full[:, None, :]
    normalized_rows = layer_normalize(alignment_block).astype(jnp.bfloat16)
    project = jnp.dot(normalized_rows, alignment_proj, preferred_element_type=jnp.float32)
    project = (project * mask_rows[:, None, :, None]).astype(jnp.bfloat16)
    inner_width = alignment_proj.shape[1] // 2
    alignment_depth = alignment_block.shape[1]
    left_side = project[..., :inner_width]
    right_side = project[..., inner_width:]

    def per_slot(operands):
        local_side, theirs = operands
        products = (
            jnp.einsum("sic,sjd->ijcd", local_side, theirs, preferred_element_type=jnp.float32)
            / alignment_depth
        )
        products = products.reshape(
            local_side.shape[1], theirs.shape[1], inner_width * inner_width
        ).astype(jnp.bfloat16)
        return jnp.dot(products, outer_proj, preferred_element_type=jnp.float32)

    update = lax.map(per_slot, (left_side, lax.all_gather(right_side, "dap", axis=2, tiled=True)))
    first_rows = rows_here[None, :] < local_chain_breaks[:, None]
    first_cols = places[None, :] < local_chain_breaks[:, None]
    same_chain = first_rows[:, :, None] == first_cols[:, None, :]
    chain_term = jnp.where(
        same_chain[..., None], chain_bias[0].astype(jnp.float32), chain_bias[1].astype(jnp.float32)
    )
    stream = pairwise_block.astype(jnp.float32) + update + chain_term
    stream = (
        stream + triangle(stream, pair_mask, outgoing_ab, outgoing_gate, outgoing_proj)
    ).astype(jnp.bfloat16)
    swapped = lax.all_to_all(stream, "dap", split_axis=2, concat_axis=1, tiled=True)
    flipped = jnp.transpose(swapped, (0, 2, 1, 3)).astype(jnp.float32)
    flipped = flipped + triangle(flipped, pair_mask, incoming_ab, incoming_gate, incoming_proj)
    flipped = (flipped * pair_mask[..., None]).astype(jnp.bfloat16)
    restored = lax.all_to_all(flipped, "dap", split_axis=2, concat_axis=1, tiled=True)
    return jnp.transpose(restored, (0, 2, 1, 3))


def pack_slots(blocks, positions, buffer_slots):
    slot_index = jnp.arange(positions.shape[0], dtype=jnp.int32)
    matches = positions[None, :] == jnp.arange(buffer_slots, dtype=jnp.int32)[:, None]
    source = jnp.sum(jnp.where(matches, slot_index[None, :], 0), axis=1)
    filled = jnp.any(matches, axis=1)
    return tuple(
        (
            jnp.where(
                filled.reshape((buffer_slots,) + (1,) * (block_array.ndim - 1)),
                jnp.take(block_array, source, axis=0),
                jnp.zeros((), block_array.dtype),
            )
            for block_array in blocks
        )
    )


def body(
    pair_rep,
    alignment,
    lengths,
    chain_breaks,
    shifts,
    alignment_proj,
    outer_proj,
    chain_bias,
    outgoing_ab,
    outgoing_gate,
    outgoing_proj,
    incoming_ab,
    incoming_gate,
    incoming_proj,
):
    weight_params = (
        alignment_proj,
        outer_proj,
        chain_bias,
        outgoing_ab,
        outgoing_gate,
        outgoing_proj,
        incoming_ab,
        incoming_gate,
        incoming_proj,
    )
    group_count = lax.axis_size("pool")
    my_group = lax.axis_index("pool")
    slot_count = pair_rep.shape[0]
    capacity = max(2, (2 * slot_count + group_count - 1) // group_count)
    buffer_slots = group_count * capacity
    starting_row = lax.axis_index("dap") * pair_rep.shape[1]
    slot_index = jnp.arange(slot_count, dtype=jnp.int32)
    earlier = (shifts[None, :] == shifts[:, None]) & (slot_index[None, :] < slot_index[:, None])
    slot_rank = jnp.sum(earlier.astype(jnp.int32), axis=1)
    send_at = (my_group + shifts) % group_count * capacity + slot_rank
    source_group = (my_group - shifts) % group_count
    receive_position = source_group * capacity + slot_rank
    home_index = my_group * slot_count + slot_index
    result = pair_update_portion(
        pair_rep,
        alignment,
        jnp.take(lengths, home_index),
        jnp.take(chain_breaks, home_index),
        starting_row,
        weight_params,
    )
    outgoing = pack_slots((result,), send_at, buffer_slots)[0]
    received_blocks = lax.all_to_all(outgoing, "pool", split_axis=0, concat_axis=0, tiled=True)
    return jnp.take(received_blocks, receive_position, axis=0)


def solution(mesh):
    return jax.shard_map(
        body,
        mesh=mesh,
        in_specs=(
            P(("screen", "pool"), "dap", None, None),
            P(("screen", "pool"), None, "dap", None),
            P("screen"),
            P("screen"),
            P("screen"),
            P(),
            P(),
            P(),
            P(),
            P(),
            P(),
            P(),
            P(),
            P(),
        ),
        out_specs=P(("screen", "pool"), "dap", None, None),
        check_vma=False,
    )
```

profile of v0, /device:TPU:0, one launch (start us, length us, event | category | flops | bytes accessed | tf_op | source)
XLA Modules:
  0.0 264.2 jit_solution(7288856007735504972)
XLA Ops:
  6.6 1.5 gather_fusion.2
  9.7 1.8 convert_reduce_fusion
  14.0 3.2 %all_gather.9 = bf16[22,16,16,32]{3,2,1,0:T(8,128)(2,1)} all-gather(bf16[22,16,8,32]{3,2,1,0:T(8,128)(2,1)S(1)} %get-tuple-element.83), channel_id=1, replica_groups=mesh['screen'=2,'pool'=8,'dap'=2] {'dap'}, dimensions={2}, use_global_device_ids=true | all-gather | bytes 540672 | tf_op jit(solution)/shard_map/all_gather | solution.py:82
  17.3 85.6 %while.10 = (s32[]{:T(128)}, f32[22,8,16,128]{3,2,1,0:T(8,128)}, bf16[22,16,16,32]{3,2,1,0:T(8,128)(2,1)}, bf16[22,16,8,32]{3,2,1,0:T(8,128)(2,1)S(1)}, bf16[1024,128]{1,0:T(8,128)(2,1)S(1)}, /*index=5*/s32[]{:T(128)}) while((s32[]{:T(128)}, f32[22,8,16,128]{3,2,1,0:T(8,128)}, bf16[22,16,16,32]{3,2,1,0:T(8,128)(2,1)}, ...), condition=%wide.region_6.8_spmd, body=%wide.region_5.7_spmd.sunk | while | flops 38010880 | bytes 1974861 | solution.py:82
  103.0 2.2 fusion.67
  107.2 1.6 fusion.28
  109.1 5.1 %copy.83 = bf16[22,8,16,128]{2,1,3,0:T(8,128)(2,1)} copy(bf16[22,8,16,128]{3,2,1,0:T(8,128)(2,1)S(1)} %get-tuple-element.80) | data formatting | bytes 1441792 | tf_op jit(solution)/shard_map/convert_element_type | solution.py:23
  114.1 2.1 fusion.10
  116.2 5.0 %all-gather.3.cloned.1.call-done = bf16[22,16,16,128]{3,2,1,0:T(8,128)(2,1)} async-done(((bf16[22,8,16,128]{3,2,1,0:T(8,128)(2,1)}), bf16[22,16,16,128]{3,2,1,0:T(8,128)(2,1)}) %all-gather.3.cloned.1.call-update) | async-done | bytes 1441808 | tf_op jit(solution)/shard_map/all_gather | solution.py:32
  121.2 10.2 %copy.82 = bf16[22,16,16,128]{2,1,3,0:T(8,128)(2,1)} copy(bf16[22,16,16,128]{3,2,1,0:T(8,128)(2,1)} %all-gather.3.cloned.1.call-done) | data formatting | bytes 2883584 | tf_op jit(solution)/shard_map/all_gather | solution.py:32
  131.4 12.2 %fusion.69 = f32[22,128,16,8]{2,3,1,0:T(8,128)} fusion(bf16[22,16,16,128]{2,1,3,0:T(8,128)(2,1)} %copy.82, bf16[22,8,16,128]{2,1,3,0:T(8,128)(2,1)} %copy.83), kind=kOutput, calls=%fused_computation.151 | convolution fusion | flops 11534336 | bytes 3604480 | tf_op jit(solution)/shard_map/sikc,sjkc->sijc/dot_general | solution.py:29
  143.6 7.3 %copy.84 = f32[22,128,16,8]{1,2,3,0:T(8,128)S(1)} copy(f32[22,128,16,8]{2,3,1,0:T(8,128)} %fusion.69) | data formatting | bytes 2883584 | tf_op jit(solution)/shard_map/sikc,sjkc->sijc/dot_general | solution.py:29
  153.6 4.3 %all_to_all.32 = bf16[22,8,16,128]{3,1,0,2:T(8,128)(2,1)S(1)} all-to-all(bf16[22,8,16,128]{3,1,0,2:T(8,128)(2,1)S(1)} %copy.85), channel_id=1, replica_groups=mesh['screen'=2,'pool'=8,'dap'=2] {'dap'}, dimensions={2} | all-to-all | bytes 1441792 | tf_op jit(solution)/shard_map/all_to_all | solution.py:93
  160.5 1.6 fusion.18
  162.6 5.1 %copy.88 = bf16[22,8,16,128]{2,1,3,0:T(8,128)(2,1)} copy(bf16[22,8,16,128]{3,2,1,0:T(8,128)(2,1)S(1)} %get-tuple-element.78) | data formatting | bytes 1441792 | tf_op jit(solution)/shard_map/convert_element_type | solution.py:23
  167.6 2.1 fusion.12
  169.7 3.4 %all-gather.5.cloned.1.call-done = bf16[22,16,16,128]{3,2,1,0:T(8,128)(2,1)} async-done(((bf16[22,8,16,128]{3,2,1,0:T(8,128)(2,1)}), bf16[22,16,16,128]{3,2,1,0:T(8,128)(2,1)}) %all-gather.5.cloned.1.call-update) | async-done | bytes 1441808 | tf_op jit(solution)/shard_map/all_gather | solution.py:32
  173.1 10.2 %copy.87 = bf16[22,16,16,128]{2,1,3,0:T(8,128)(2,1)} copy(bf16[22,16,16,128]{3,2,1,0:T(8,128)(2,1)} %all-gather.5.cloned.1.call-done) | data formatting | bytes 2883584 | tf_op jit(solution)/shard_map/all_gather | solution.py:32
  183.3 12.2 %fusion.70 = f32[22,128,16,8]{2,3,1,0:T(8,128)} fusion(bf16[22,16,16,128]{2,1,3,0:T(8,128)(2,1)} %copy.87, bf16[22,8,16,128]{2,1,3,0:T(8,128)(2,1)} %copy.88), kind=kOutput, calls=%fused_computation.152 | convolution fusion | flops 11534336 | bytes 3604480 | tf_op jit(solution)/shard_map/sikc,sjkc->sijc/dot_general | solution.py:29
  195.5 7.3 %copy.89 = f32[22,128,16,8]{1,2,3,0:T(8,128)S(1)} copy(f32[22,128,16,8]{2,3,1,0:T(8,128)} %fusion.70) | data formatting | bytes 2883584 | tf_op jit(solution)/shard_map/sikc,sjkc->sijc/dot_general | solution.py:29
  205.7 4.3 %all_to_all.33 = bf16[22,8,16,128]{3,1,0,2:T(8,128)(2,1)S(1)} all-to-all(bf16[22,8,16,128]{3,1,0,2:T(8,128)(2,1)S(1)} %copy.90), channel_id=1, replica_groups=mesh['screen'=2,'pool'=8,'dap'=2] {'dap'}, dimensions={2} | all-to-all | bytes 1441792 | tf_op jit(solution)/shard_map/all_to_all | solution.py:97
  211.2 1.4 select_select_fusion
  212.6 5.8 %all-to-all-start.2 = ((bf16[48,8,16,128]{3,2,1,0:T(8,128)(2,1)}), bf16[48,8,16,128]{3,2,1,0:T(8,128)(2,1)S(1)}, u32[]{:S(2)}, u32[]{:S(2)}) async-start(bf16[48,8,16,128]{3,2,1,0:T(8,128)(2,1)} %select_select_fusion), calls=%async_computation.2 | async-start | bytes 3145728 | tf_op jit(solution)/shard_map/all_to_all | solution.py:167
  218.5 37.3 %all-to-all-done.2 = bf16[48,8,16,128]{3,2,1,0:T(8,128)(2,1)S(1)} async-done(((bf16[48,8,16,128]{3,2,1,0:T(8,128)(2,1)}), bf16[48,8,16,128]{3,2,1,0:T(8,128)(2,1)S(1)}, u32[]{:S(2)}, u32[]{:S(2)}) %all-to-all-start.2) | async-done | bytes 1572896 | tf_op jit(solution)/shard_map/all_to_all | solution.py:167
  (217 shorter events, 102.7 us)
Async XLA Ops:
  6.5 99.7 %copy-start = (bf16[128,512]{1,0:T(8,128)(2,1)S(1)}, bf16[128,512]{1,0:T(8,128)(2,1)}, u32[]{:S(2)}) copy-start(bf16[128,512]{1,0:T(8,128)(2,1)} %param.26) | copy-start | bytes 393220
  6.5 114.7 %all-gather.3.cloned.1.call-start = ((), (), s32[]{:S(2)}) async-start(), calls=%async_computation.3 | async-start | bytes 2162688 | tf_op jit(solution)/shard_map/all_gather | solution.py:32
  6.6 5.0 %copy-start.3 = (bf16[22,16,8,256]{3,2,1,0:T(8,128)(2,1)S(1)}, bf16[22,16,8,256]{3,2,1,0:T(8,128)(2,1)}, u32[]{:S(2)}) copy-start(bf16[22,16,8,256]{3,2,1,0:T(8,128)(2,1)} %param.19) | copy-start | bytes 4325380
  11.5 1.0 copy-start.11
  14.0 3.3 %copy-start.2 = (bf16[1024,128]{1,0:T(8,128)(2,1)S(1)}, bf16[1024,128]{1,0:T(8,128)(2,1)}, u32[]{:S(2)}) copy-start(bf16[1024,128]{1,0:T(8,128)(2,1)} %param.24) | copy-start | bytes 786436
  17.3 85.6 %copy-start.9 = (bf16[2,128]{1,0:T(2,128)(2,1)S(1)}, bf16[2,128]{1,0:T(2,128)(2,1)}, u32[]{:S(2)}) copy-start(bf16[2,128]{1,0:T(2,128)(2,1)} %param.25) | copy-start | bytes 1540
  108.8 64.3 %all-gather.5.cloned.1.call-start = ((), (), s32[]{:S(2)}) async-start(), calls=%async_computation.4 | async-start | bytes 2162688 | tf_op jit(solution)/shard_map/all_gather | solution.py:32
  109.1 5.1 %copy-start.12 = (bf16[128,128]{1,0:T(8,128)(2,1)S(1)}, bf16[128,128]{1,0:T(8,128)(2,1)}, u32[]{:S(2)}) copy-start(bf16[128,128]{1,0:T(8,128)(2,1)} %param.27) | copy-start | bytes 98308
  150.9 1.4 copy-start.4
  150.9 1.4 copy-start.7
  158.1 1.4 copy-start.6
  160.5 1.7 copy-start.10
  162.6 5.1 %copy-start.13 = (bf16[128,128]{1,0:T(8,128)(2,1)S(1)}, bf16[128,128]{1,0:T(8,128)(2,1)}, u32[]{:S(2)}) copy-start(bf16[128,128]{1,0:T(8,128)(2,1)} %param.30) | copy-start | bytes 98308
  202.8 1.4 copy-start.5
  202.8 1.4 copy-start.8
  212.6 43.1 %all-to-all-start.2 = ((bf16[48,8,16,128]{3,2,1,0:T(8,128)(2,1)}), bf16[48,8,16,128]{3,2,1,0:T(8,128)(2,1)S(1)}, u32[]{:S(2)}, u32[]{:S(2)}) async-start(bf16[48,8,16,128]{3,2,1,0:T(8,128)(2,1)} %select_select_fusion), calls=%async_computation.2 | async-start | bytes 3145728 | tf_op jit(solution)/shard_map/all_to_all | solution.py:167
  218.4 39.0 %copy-start.1 = (bf16[128,512]{1,0:T(8,128)(2,1)S(1)}, bf16[128,512]{1,0:T(8,128)(2,1)}, u32[]{:S(2)}) copy-start(bf16[128,512]{1,0:T(8,128)(2,1)} %param.26) | copy-start | bytes 393220
Sparse Core Ops, SparseCore 0:
  109.0 12.1 all-gather.2
  162.3 10.7 all-gather.4
where the time goes:
time: 266 us; the launch traced here: 264 us
  local copies, waits for them, and re-layouts  107 us (40%)
  matrix products  62.7 us (24%)
  waiting for transfers between devices  45.7 us (17%)
  other arithmetic  16.5 us (6%)
  between operations  13.9 us (5%)
  blocking collectives  11.9 us (4%)
  starting transfers between devices  6.01 us (2%)
    convert_element_type x44, local copies, waits for them, and re-layouts, per_slot(): products = products.reshape(local_side.shape[1], theirs.shape[1], inner_w...  37.8 us
    all_to_all x1, waiting for transfers between devices, body(): lax.all_to_all(outgoing, 'pool', split_axis=0, concat_axis=0, tiled=True)  37.3 us
    dot_general x2, matrix products, triangle(): jnp.einsum('sikc,sjkc->sijc', left_side, lax.all_gather(right_side, 'dap'...  24.4 us
    all_gather x2, local copies, waits for them, and re-layouts, triangle(): lax.all_gather(right_side, 'dap', axis=1, tiled=True)  20.4 us
    dynamic_slice x44, local copies, waits for them, and re-layouts, pair_update_portion(): lax.map(per_slot, (left_side, lax.all_gather(right_side, 'dap', axis=2, t...  18.6 us
    dot_general x22, matrix products, per_slot(): return jnp.dot(products, outer_proj, preferred_element_type=jnp.float32)  18.5 us
    dot_general x2, local copies, waits for them, and re-layouts, triangle(): jnp.einsum('sikc,sjkc->sijc', left_side, lax.all_gather(right_side, 'dap'...  14.6 us
    convert_element_type x2, local copies, waits for them, and re-layouts, triangle(): left_side = (left_side * pair_mask[..., None]).astype(jnp.bfloat16)  10.1 us
  transfers between devices with their start and end apart: 3, of which 3 were waited for; matrix products, arithmetic and copies ran while one was open for 6% of the time, Pallas kernels for 0%

commit v1 on v0

v1 whole, which is shorter than its diff:
```python
import functools

import jax
import jax.numpy as jnp
from jax import lax
from jax.experimental import pallas as pl
from jax.experimental.pallas import tpu as pltpu
from jax.sharding import PartitionSpec as P

EPSILON = 1e-05
F32 = jnp.float32
BF16 = jnp.bfloat16


def dot(left, right):
    return jnp.dot(left, right, preferred_element_type=F32)


def sigmoid(values):
    return 0.5 * jnp.tanh(0.5 * values) + 0.5


def normalize(values):
    center = jnp.mean(values, axis=-1, keepdims=True)
    values = values - center
    spread = jnp.mean(values * values, axis=-1, keepdims=True)
    return (values * lax.rsqrt(spread + EPSILON)).astype(BF16)


def update_kernel(
    half_ref,
    lengths_ref,
    breaks_ref,
    own_pair,
    other_pair,
    own_alignment,
    other_alignment,
    w_project,
    w_spread,
    w_outer,
    bias,
    out_w,
    out_proj,
    in_w,
    in_proj,
    keep_ref,
    send_ref,
    side,
    rights,
    spread,
    stacked,
    outer,
    stream,
    first,
    second,
):
    count, rows, full, width = own_pair.shape
    depth = own_alignment.shape[1]
    pairs = full * full
    inner = rights.shape[-1] // depth
    half = half_ref[0]

    lane = lax.broadcasted_iota(jnp.int32, (1, 128), 1)
    groups = [(lane // inner) == q for q in range(4)]

    def project(step, carry):
        length = lengths_ref[step]
        for place, ref in ((half, own_alignment), (1 - half, other_alignment)):
            values = ref[step].astype(F32).reshape(depth * rows, ref.shape[-1])
            values = dot(normalize(values), w_project[...])
            residue = (
                lax.broadcasted_iota(jnp.int32, (depth, rows, 1), 1) + place * rows
            ).reshape(depth * rows, 1)
            values = jnp.where(residue < length, values, 0.0).astype(BF16).astype(F32)
            left = values[:, :128] * (1.0 / depth)
            side[step, place] = left
            right = values[:, 128:].reshape(depth, rows, 128)
            for group in range(depth // 4):
                piece = right[4 * group]
                for q in range(1, 4):
                    piece = jnp.where(groups[q], right[4 * group + q], piece)
                rights[step, pl.ds(pl.multiple_of(place * rows, rows), rows), 128 * group : 128 * group + 128] = piece
        return carry

    lax.fori_loop(0, count, project, 0)

    flat = rights[...].reshape(count * full, rights.shape[-1]).astype(BF16)
    spread[...] = dot(flat, w_spread[...]).astype(BF16).reshape(spread.shape)
    stacked[...] = jnp.zeros_like(stacked)

    row = lax.broadcasted_iota(jnp.int32, (pairs, 1), 0)
    row_i = row // full
    row_j = row % full

    def complex_step(step, carry):
        length = lengths_ref[step]
        stop = breaks_ref[step]
        for i in range(full):
            left = side[step, i // rows, pl.ds(i % rows, depth, stride=rows), :]
            for q in range(4):
                stacked[16 * q : 16 * q + 16, 128 * i : 128 * i + 128] = jnp.where(
                    groups[q], left, 0.0
                ).astype(BF16)
        right = spread[step]
        right = jnp.concatenate([right[:, 128 * g : 128 * g + 128] for g in range(8)], axis=0)
        for i in range(0, full, 2):
            product = dot(right, stacked[:, 128 * i : 128 * i + 256]).astype(BF16)
            for g in range(8):
                outer[16 * i : 16 * i + 16, 128 * g : 128 * g + 128] = product[16 * g : 16 * g + 16, :128]
                outer[16 * i + 16 : 16 * i + 32, 128 * g : 128 * g + 128] = product[16 * g : 16 * g + 16, 128:]
        stream[pl.ds(pl.multiple_of(half * rows * full, rows * full), rows * full), :] = (
            own_pair[step].astype(F32).reshape(rows * full, width)
        )
        stream[pl.ds(pl.multiple_of((1 - half) * rows * full, rows * full), rows * full), :] = (
            other_pair[step].astype(F32).reshape(rows * full, width)
        )
        same = (row_i < stop) == (row_j < stop)
        inside = ((row_i < length) & (row_j < length)).astype(F32)
        z1 = stream[...] + dot(outer[...], w_outer[...])
        z1 = z1 + jnp.where(same, bias[0:1].astype(F32), bias[1:2].astype(F32))

        def sides(values, weight):
            x = normalize(values)
            projected = dot(x, weight[...])
            a = sigmoid(projected[:, 128:256]) * projected[:, :128] * inside
            b = sigmoid(projected[:, 384:512]) * projected[:, 256:384] * inside
            gate = sigmoid(projected[:, 512:])
            return a.astype(BF16).astype(F32), b.astype(BF16).astype(F32), gate

        def contract(rows_of, columns):
            parts = []
            for i in range(full):
                total = None
                for k in range(full):
                    term = rows_of(i, k) * columns[k]
                    total = term if total is None else total + term
                parts.append(total)
            return jnp.concatenate(parts, axis=0)

        a, b, gate = sides(z1, out_w)
        first[...] = a
        second[...] = b
        columns = [second[pl.ds(k, full, stride=full), :] for k in range(full)]
        t = contract(lambda i, k: first[pl.ds(full * i + k, 1), :], columns)
        z2 = (z1 + gate * dot(normalize(t), out_proj[...])).astype(BF16).astype(F32)
        a, b, gate = sides(z2, in_w)
        second[...] = b
        columns = [a[full * k : full * k + full] for k in range(full)]
        t = contract(lambda i, k: second[pl.ds(full * k + i, 1), :], columns)
        stream[...] = (z2 + gate * dot(normalize(t), in_proj[...])) * inside
        keep_ref[step] = (
            stream[pl.ds(pl.multiple_of(half * rows * full, rows * full), rows * full), :]
            .reshape(rows, full, width)
            .astype(BF16)
        )
        send_ref[step] = (
            stream[pl.ds(pl.multiple_of((1 - half) * rows * full, rows * full), rows * full), :]
            .reshape(rows, full, width)
            .astype(BF16)
        )
        return carry

    lax.fori_loop(0, count, complex_step, 0)


def update(half, lengths, breaks, own_pair, other_pair, own_alignment, other_alignment, weights):
    (
        alignment_proj,
        outer_proj,
        chain_bias,
        outgoing_ab,
        outgoing_gate,
        outgoing_proj,
        incoming_ab,
        incoming_gate,
        incoming_proj,
    ) = weights
    count, rows, full, width = own_pair.shape
    depth = own_alignment.shape[1]
    inner = alignment_proj.shape[1] // 2
    pieces = 128 // inner
    sets = inner // pieces
    w_project = jnp.concatenate(
        [alignment_proj[:, :inner]] * pieces + [alignment_proj[:, inner:]] * pieces, axis=1
    )
    source = lax.broadcasted_iota(jnp.int32, (depth * inner, sets * 128), 0)
    target = lax.broadcasted_iota(jnp.int32, (depth * inner, sets * 128), 1)
    r, c2 = source // inner, source % inner
    w_spread = (target == (c2 // pieces) * 128 + (c2 % pieces) * depth + r).astype(BF16)
    w_outer = (
        outer_proj.reshape(inner, inner, width).transpose(1, 0, 2).reshape(inner * inner, width)
    )
    out_w = jnp.concatenate([outgoing_ab, outgoing_gate], axis=1)
    in_w = jnp.concatenate([incoming_ab, incoming_gate], axis=1)
    smem = pl.BlockSpec(memory_space=pltpu.SMEM)
    vmem = pl.BlockSpec(memory_space=pltpu.VMEM)
    shape = jax.ShapeDtypeStruct(own_pair.shape, BF16)
    pairs = full * full
    return pl.pallas_call(
        update_kernel,
        out_shape=(shape, shape),
        in_specs=[smem] * 3 + [vmem] * 12,
        out_specs=(vmem, vmem),
        scratch_shapes=[
            pltpu.VMEM((count, 2, depth * rows, 128), F32),
            pltpu.VMEM((count, full, depth * inner), F32),
            pltpu.VMEM((count, full, sets * 128), BF16),
            pltpu.VMEM((128, full * 128), BF16),
            pltpu.VMEM((pairs, inner * inner), BF16),
            pltpu.VMEM((pairs, width), F32),
            pltpu.VMEM((pairs, width), F32),
            pltpu.VMEM((pairs, width), F32),
        ],
        name="pair_update",
    )(
        half,
        lengths,
        breaks,
        own_pair,
        other_pair,
        own_alignment,
        other_alignment,
        w_project,
        w_spread,
        w_outer,
        chain_bias,
        out_w,
        outgoing_proj,
        in_w,
        incoming_proj,
    )


def pack_slots(blocks, positions, buffer_slots):
    slot_index = jnp.arange(positions.shape[0], dtype=jnp.int32)
    matches = positions[None, :] == jnp.arange(buffer_slots, dtype=jnp.int32)[:, None]
    source = jnp.sum(jnp.where(matches, slot_index[None, :], 0), axis=1)
    return jnp.take(blocks, source, axis=0)


def body(pair_rep, alignment, lengths, chain_breaks, shifts, *weights):
    group_count = lax.axis_size("pool")
    my_group = lax.axis_index("pool")
    half = lax.axis_index("dap")
    slot_count = pair_rep.shape[0]
    count = slot_count // 2
    capacity = max(2, (2 * slot_count + group_count - 1) // group_count)
    buffer_slots = group_count * capacity
    swap = [(0, 1), (1, 0)]
    mine = half * count
    theirs = (1 - half) * count
    other_pair = lax.ppermute(lax.dynamic_slice_in_dim(pair_rep, theirs, count), "dap", swap)
    other_alignment = lax.ppermute(lax.dynamic_slice_in_dim(alignment, theirs, count), "dap", swap)
    home = my_group * slot_count + mine
    keep, send = update(
        half.reshape(1).astype(jnp.int32),
        lax.dynamic_slice_in_dim(lengths, home, count),
        lax.dynamic_slice_in_dim(chain_breaks, home, count),
        lax.dynamic_slice_in_dim(pair_rep, mine, count),
        other_pair,
        lax.dynamic_slice_in_dim(alignment, mine, count),
        other_alignment,
        weights,
    )
    received = lax.ppermute(send, "dap", swap)
    result = jnp.concatenate([keep, received], axis=0)

    slot_index = jnp.arange(slot_count, dtype=jnp.int32)
    earlier = (shifts[None, :] == shifts[:, None]) & (slot_index[None, :] < slot_index[:, None])
    slot_rank = jnp.sum(earlier.astype(jnp.int32), axis=1)
    send_at = (my_group + shifts) % group_count * capacity + slot_rank
    send_at = jnp.where(half == 0, send_at, jnp.roll(send_at, count))
    receive_position = (my_group - shifts) % group_count * capacity + slot_rank
    outgoing = pack_slots(result, send_at, buffer_slots)
    received_blocks = lax.all_to_all(outgoing, "pool", split_axis=0, concat_axis=0, tiled=True)
    return jnp.take(received_blocks, receive_position, axis=0)


def solution(mesh):
    return jax.shard_map(
        body,
        mesh=mesh,
        in_specs=(
            P(("screen", "pool"), "dap", None, None),
            P(("screen", "pool"), None, "dap", None),
            P("screen"),
            P("screen"),
            P("screen"),
        )
        + (P(),) * 9,
        out_specs=P(("screen", "pool"), "dap", None, None),
        check_vma=False,
    )
```

time: 266 us -> 92.4 us (0.35)
  local copies, waits for them, and re-layouts: 107 us -> 9.01 us
  matrix products: 62.7 us -> 0 us
  Pallas kernels: 0 us -> 29.8 us
  between operations: 13.9 us -> 0.13 us
  blocking collectives: 11.9 us -> 0 us
  other arithmetic: 16.5 us -> 6.15 us
  waiting for transfers between devices: 45.7 us -> 38.8 us
    dot_general x53 -> x0, matrix products: 62.7 us -> none  [the longest x2 24.4 us: triangle(): jnp.einsum('sikc,sjkc->sijc', left_side, lax.all_gather(right_side, 'dap'...]
    convert_element_type x48 -> x0, local copies, waits for them, and re-layouts: 48.3 us -> none  [the longest x44 37.8 us: per_slot(): products = products.reshape(local_side.shape[1], theirs.shape[1], inner_w...]
    pallas_call x0 -> x1, Pallas kernels: none -> 29.8 us  [update(): pl.pallas_call(update_kernel, out_shape=(shape, shape), in_specs=[smem] *...]
    all_gather x2 -> x0, local copies, waits for them, and re-layouts: 20.4 us -> none  [triangle(): lax.all_gather(right_side, 'dap', axis=1, tiled=True)]
    dot_general x2 -> x0, local copies, waits for them, and re-layouts: 14.6 us -> none  [triangle(): jnp.einsum('sikc,sjkc->sijc', left_side, lax.all_gather(right_side, 'dap'...]
    dynamic_slice x44 -> x4, local copies, waits for them, and re-layouts: 18.6 us -> 4.49 us  [the longest x1 2.37 us: body(): lax.dynamic_slice_in_dim(alignment, theirs, count)]
    reduce_sum x10 -> x0, other arithmetic: 9.72 us -> none  [the longest x5 5.38 us: layer_normalize(): center = jnp.mean(values, axis=-1, keepdims=True)]
    all_to_all x2 -> x0, blocking collectives: 8.63 us -> none  [the longest x1 4.31 us: pair_update_portion(): lax.all_to_all(stream, 'dap', split_axis=2, concat_axis=1, tiled=True)]
  transfers between devices with their start and end apart: 3 -> 4, of which waited for: 3 -> 2; matrix products, arithmetic and copies ran while one was open for 6% -> 7% of each run, Pallas kernels for 0% -> 0%
where the time goes in v1:
time: 92.4 us; the launch traced here: 92.2 us
  waiting for transfers between devices  38.8 us (42%)
  Pallas kernels  29.8 us (32%)
  local copies, waits for them, and re-layouts  9.01 us (10%)
  starting transfers between devices  8.29 us (9%)
  other arithmetic  6.15 us (7%)
    all_to_all x1, waiting for transfers between devices, body(): lax.all_to_all(outgoing, 'pool', split_axis=0, concat_axis=0, tiled=True)  37.3 us
    pallas_call x1, Pallas kernels, update(): pl.pallas_call(update_kernel, out_shape=(shape, shape), in_specs=[smem] *...  29.8 us
    all_to_all x1, starting transfers between devices, body(): lax.all_to_all(outgoing, 'pool', split_axis=0, concat_axis=0, tiled=True)  7.11 us
    dynamic_slice x1, local copies, waits for them, and re-layouts, body(): lax.dynamic_slice_in_dim(alignment, theirs, count)  2.37 us
  transfers between devices with their start and end apart: 4, of which 2 were waited for; matrix products, arithmetic and copies ran while one was open for 7% of the time, Pallas kernels for 0%

profile of v1, /device:TPU:0, one launch (start us, length us, event | category | flops | bytes accessed | tf_op | source)
XLA Modules:
  0.0 92.2 jit_solution(17278278349598492661)
XLA Ops:
  0.0 2.4 %constant_dynamic-slice_fusion = (bf16[11,16,8,256]{3,2,1,0:T(8,128)(2,1)S(1)}, bf16[11,16,8,256]{3,2,1,0:T(8,128)(2,1)}) fusion(bf16[22,16,8,256]{3,2,1,0:T(8,128)(2,1)} %param.15, s32[]{:T(128)S(6)} %select_n.91, s32[]{:T(128)S(6)} %select_n.90), kind=kLoop, calls=%fused_computation.53 | loop fusion | bytes 2883592 | tf_op jit(solution)/shard_map/dynamic_slice | solution.py:253
  2.4 0.6 collective-permute-start.1
  3.0 0.9 constant_dynamic-slice_fusion.2
  3.9 0.6 dynamic_slice.18.lengths_ref
  4.5 0.6 dynamic_slice.19.breaks_ref
  5.2 0.1 copy.19
  5.4 0.8 copy.22
  6.2 0.2 convert_reduce_fusion
  6.5 0.1 select_reduce_fusion
  6.6 0.9 concatenate.17.w_project
  7.5 0.8 pad_maximum_fusion.1
  8.3 1.5 %fusion.9.w_spread = bf16[512,1024]{1,0:T(8,128)(2,1)} fusion(s32[512]{0:T(512)S(1)} %get-tuple-element.19, s32[512]{0:T(512)S(1)} %get-tuple-element.22, s32[512]{0:T(512)S(1)} %get-tuple-element.20, s32[512]{0:T(512)S(1)} %get-tuple-element.21, pred[512]{0:T(512)(128)(4,1)S(1)} %get-tuple-element.23, pred[512]{0:T(512)(128)(4,1)S(1)} %get-tuple-element.24), kind=kLoop, calls=%fused_computation.19 | loop fusion | flops 14155776 | bytes 1057792 | tf_op jit(solution)/shard_map/convert_element_type | solution.py:189
  9.9 0.7 copy-done.2
  10.6 0.3 copy-done
  10.9 29.8 %pair_update.1 = (bf16[11,8,16,128]{3,2,1,0:T(8,128)(2,1)}, bf16[11,8,16,128]{3,2,1,0:T(8,128)(2,1)}) custom-call(s32[1]{0:T(128)} %bitcast.half_ref, s32[11]{0:T(128)} %dynamic_slice.18.lengths_ref, s32[11]{0:T(128)} %dynamic_slice.19.breaks_ref, bf16[11,8,16,128]{3,2,1,0:T(8,128)(2,1)} %get-tuple-element.14.own_pair, bf16[11,8,16,128]{3,2,1,0:T(8,128)(2,1)} %copy-done.2, ...), custom_call_target="tpu_custom_call" | custom-call | tf_op jit(solution)/shard_map/pair_update/pallas_call | solution.py:199
  40.7 0.6 collective-permute-start.2
  41.3 1.5 %collective-permute-done.2 = bf16[11,8,16,128]{3,2,1,0:T(8,128)(2,1)S(1)} collective-permute-done((bf16[11,8,16,128]{3,2,1,0:T(8,128)(2,1)}, bf16[11,8,16,128]{3,2,1,0:T(8,128)(2,1)S(1)}, u32[]{:S(2)}, u32[]{:S(2)}) %collective-permute-start.2) | collective-permute-done | bytes 360480 | tf_op jit(solution)/shard_map/ppermute | solution.py:265
  42.8 1.0 %pad_maximum_fusion = bf16[22,8,16,128]{3,2,1,0:T(8,128)(2,1)S(1)} fusion(bf16[11,8,16,128]{3,2,1,0:T(8,128)(2,1)S(1)} %collective-permute-done.2, bf16[11,8,16,128]{3,2,1,0:T(8,128)(2,1)} %get-tuple-element.7), kind=kLoop, calls=%fused_computation.21 | loop fusion | flops 360448 | bytes 1441792 | tf_op jit(solution)/shard_map/concatenate | solution.py:266
  43.8 0.8 gather_fusion
  44.7 1.4 %broadcast_select_fusion = bf16[48,8,16,128]{3,2,1,0:T(8,128)(2,1)} fusion(bf16[48,8,16,128]{3,2,1,0:T(8,128)(2,1)S(1)} %gather_fusion, pred[48]{0:T(512)(128)(4,1)S(1)} %compare_and_fusion), kind=kLoop, calls=%fused_computation.20 | loop fusion | flops 786432 | bytes 3145776 | tf_op jit(solution)/shard_map/jit(_take)/select_n | solution.py:238
  46.0 7.1 %all-to-all-start = ((bf16[48,8,16,128]{3,2,1,0:T(8,128)(2,1)}), bf16[48,8,16,128]{3,2,1,0:T(8,128)(2,1)S(1)}, u32[]{:S(2)}, u32[]{:S(2)}) async-start(bf16[48,8,16,128]{3,2,1,0:T(8,128)(2,1)} %broadcast_select_fusion), calls=%async_computation | async-start | bytes 3145728 | tf_op jit(solution)/shard_map/all_to_all | solution.py:275
  53.2 37.3 %all-to-all-done = bf16[48,8,16,128]{3,2,1,0:T(8,128)(2,1)S(1)} async-done(((bf16[48,8,16,128]{3,2,1,0:T(8,128)(2,1)}), bf16[48,8,16,128]{3,2,1,0:T(8,128)(2,1)S(1)}, u32[]{:S(2)}, u32[]{:S(2)}) %all-to-all-start) | async-done | bytes 1572896 | tf_op jit(solution)/shard_map/all_to_all | solution.py:275
  90.5 0.7 gather_fusion.1
  91.2 1.0 %broadcast_select_fusion.1 = bf16[22,8,16,128]{3,2,1,0:T(8,128)(2,1)} fusion(bf16[22,8,16,128]{3,2,1,0:T(8,128)(2,1)S(1)} %gather_fusion.1, pred[22]{0:T(512)(128)(4,1)S(1)} %get-tuple-element.9), kind=kLoop, calls=%fused_computation.22 | loop fusion | flops 360448 | bytes 1441814 | tf_op jit(solution)/shard_map/jit(_take)/select_n | solution.py:276
  (37 shorter events, 0.4 us)
Async XLA Ops:
  0.0 3.0 %copy-start.1 = (bf16[22,8,16,128]{3,2,1,0:T(8,128)(2,1)S(1)}, bf16[22,8,16,128]{3,2,1,0:T(8,128)(2,1)}, u32[]{:S(2)}) copy-start(bf16[22,8,16,128]{3,2,1,0:T(8,128)(2,1)} %param.14) | copy-start | bytes 2162692
  0.0 3.9 %copy-start.10 = (s32[176]{0:T(256)S(1)}, s32[176]{0:T(256)}, u32[]{:S(2)}) copy-start(s32[176]{0:T(256)} %param.16) | copy-start | bytes 2116
  0.0 4.5 %copy-start.11 = (s32[176]{0:T(256)S(1)}, s32[176]{0:T(256)}, u32[]{:S(2)}) copy-start(s32[176]{0:T(256)} %param.17) | copy-start | bytes 2116
  0.0 5.2 %copy-start.6 = (bf16[256,64]{0,1:T(8,128)(2,1)S(1)}, bf16[256,64]{0,1:T(8,128)(2,1)}, u32[]{:S(2)}) copy-start(bf16[256,64]{0,1:T(8,128)(2,1)} %param.19) | copy-start | bytes 98308
  2.4 3.0 %copy-start.3 = (bf16[1024,128]{1,0:T(8,128)(2,1)S(1)}, bf16[1024,128]{1,0:T(8,128)(2,1)}, u32[]{:S(2)}) copy-start(bf16[1024,128]{1,0:T(8,128)(2,1)} %param.20) | copy-start | bytes 786436
  2.4 3.8 %copy-start.9 = (s32[22]{0:T(128)S(1)}, s32[22]{0:T(128)}, u32[]{:S(2)}) copy-start(s32[22]{0:T(128)} %param.18) | copy-start | bytes 268
  2.4 5.1 %copy-start.4 = (bf16[128,512]{1,0:T(8,128)(2,1)S(1)}, bf16[128,512]{1,0:T(8,128)(2,1)}, u32[]{:S(2)}) copy-start(bf16[128,512]{1,0:T(8,128)(2,1)} %param.22) | copy-start | bytes 393220
  2.4 5.1 %copy-start.5 = (bf16[128,512]{1,0:T(8,128)(2,1)S(1)}, bf16[128,512]{1,0:T(8,128)(2,1)}, u32[]{:S(2)}) copy-start(bf16[128,512]{1,0:T(8,128)(2,1)} %param.25) | copy-start | bytes 393220
  2.4 5.1 %copy-start.7 = (bf16[128,128]{1,0:T(8,128)(2,1)S(1)}, bf16[128,128]{1,0:T(8,128)(2,1)}, u32[]{:S(2)}) copy-start(bf16[128,128]{1,0:T(8,128)(2,1)} %param.23) | copy-start | bytes 98308
  2.4 5.1 %copy-start.8 = (bf16[128,128]{1,0:T(8,128)(2,1)S(1)}, bf16[128,128]{1,0:T(8,128)(2,1)}, u32[]{:S(2)}) copy-start(bf16[128,128]{1,0:T(8,128)(2,1)} %param.26) | copy-start | bytes 98308
  2.4 7.4 %collective-permute-start.1 = (bf16[11,16,8,256]{3,2,1,0:T(8,128)(2,1)S(1)}, bf16[11,16,8,256]{3,2,1,0:T(8,128)(2,1)S(1)}, u32[]{:S(2)}, u32[]{:S(2)}) collective-permute-start(bf16[11,16,8,256]{3,2,1,0:T(8,128)(2,1)S(1)} %get-tuple-element.11), channel_id=1, source_target_pairs={{0,1},{1,0},{2,3},{3,2},{4,5},{5,4},{6,7},{7,6},{8,9},{9,8},{10,11... | collective-permute-start | bytes 2162696 | tf_op jit(solution)/shard_map/ppermute | solution.py:253
  3.9 5.9 %collective-permute-start = (bf16[11,8,16,128]{3,2,1,0:T(8,128)(2,1)S(1)}, bf16[11,8,16,128]{3,2,1,0:T(8,128)(2,1)S(1)}, u32[]{:S(2)}, u32[]{:S(2)}) collective-permute-start(bf16[11,8,16,128]{3,2,1,0:T(8,128)(2,1)S(1)} %get-tuple-element.13), channel_id=1, source_target_pairs={{0,1},{1,0},{2,3},{3,2},{4,5},{5,4},{6,7},{7,6},{8,9},{9,8},{10,11... | collective-permute-start | bytes 1081352 | tf_op jit(solution)/shard_map/ppermute | solution.py:252
  9.8 0.7 copy-start.2
  9.9 1.0 %copy-start = (bf16[11,16,8,256]{3,2,1,0:T(8,128)(2,1)}, bf16[11,16,8,256]{3,2,1,0:T(8,128)(2,1)S(1)}, u32[]{:S(2)}) copy-start(bf16[11,16,8,256]{3,2,1,0:T(8,128)(2,1)S(1)} %collective-permute-done.1.other_alignment) | copy-start | bytes 2162692
  40.7 2.1 %collective-permute-start.2 = (bf16[11,8,16,128]{3,2,1,0:T(8,128)(2,1)}, bf16[11,8,16,128]{3,2,1,0:T(8,128)(2,1)S(1)}, u32[]{:S(2)}, u32[]{:S(2)}) collective-permute-start(bf16[11,8,16,128]{3,2,1,0:T(8,128)(2,1)} %get-tuple-element.8), channel_id=1, source_target_pairs={{0,1},{1,0},{2,3},{3,2},{4,5},{5,4},{6,7},{7,6},{8,9},{9,8},{10,11... | collective-permute-start | bytes 1081352 | tf_op jit(solution)/shard_map/ppermute | solution.py:265
  46.0 44.4 %all-to-all-start = ((bf16[48,8,16,128]{3,2,1,0:T(8,128)(2,1)}), bf16[48,8,16,128]{3,2,1,0:T(8,128)(2,1)S(1)}, u32[]{:S(2)}, u32[]{:S(2)}) async-start(bf16[48,8,16,128]{3,2,1,0:T(8,128)(2,1)} %broadcast_select_fusion), calls=%async_computation | async-start | bytes 3145728 | tf_op jit(solution)/shard_map/all_to_all | solution.py:275

commit v2 on v1

v2 whole, which is shorter than its diff:
```python
import functools

import jax
import jax.numpy as jnp
import numpy as np
from jax import lax
from jax.experimental import pallas as pl
from jax.experimental.pallas import tpu as pltpu
from jax.sharding import PartitionSpec as P

EPSILON = 1e-05
F32 = jnp.float32
BF16 = jnp.bfloat16
LANES = 128


def dot(left, right):
    return jnp.dot(left, right, preferred_element_type=F32)


def normalize(values, scale):
    width = values.shape[-1]
    values = values - jnp.sum(values, axis=-1, keepdims=True) * (1.0 / width)
    spread = jnp.sum(values * values, axis=-1, keepdims=True)
    return (values * (lax.rsqrt(spread + width * EPSILON) * scale)).astype(BF16)


def lane_groups(inner):
    group = lax.broadcasted_iota(jnp.int32, (1, LANES), 1) // inner
    return [group == q for q in range(LANES // inner)]


def project_kernel(send, place_ref, lengths_ref, *refs):
    if send:
        alignment, pair, w_align, w_spread, out_ref, pair_out, rows_in, side, rights, sems = refs
    else:
        alignment, w_align, w_spread, out_ref, rows_in, side, rights, sems = refs
    count, depth, rows, width = rows_in.shape
    inner = rights.shape[-1] // depth
    pieces = LANES // inner
    half = place_ref[0]
    start = place_ref[1] if send else place_ref[2]
    home = place_ref[3]
    copy = pltpu.make_async_copy(alignment.at[pl.ds(start, count)], rows_in, sems.at[0])
    copy.start()
    if send:
        pair_copy = pltpu.make_async_copy(pair.at[pl.ds(start, count)], pair_out, sems.at[1])
        pair_copy.start()
    groups = lane_groups(inner)
    source = lax.broadcasted_iota(jnp.int32, (2 * inner, 2 * LANES), 0)
    target = lax.broadcasted_iota(jnp.int32, (2 * inner, 2 * LANES), 1)
    repeat = (source == (target // LANES) * inner + target % inner).astype(BF16)
    w_project = dot(w_align[...], repeat).astype(BF16)
    copy.wait()

    def step(index, carry):
        length = lengths_ref[home + start + index]
        values = rows_in[index].astype(F32).reshape(depth * rows, width)
        values = dot(normalize(values, width**0.5), w_project)
        residue = lax.broadcasted_iota(jnp.int32, (rows, 1), 0) + half * rows
        mask = jnp.where(residue < length, 1.0, 0.0)
        values = values.reshape(depth, rows, 2 * LANES) * mask
        side[...] = values[:, :, :LANES].reshape(depth * rows, LANES) * (1.0 / depth)
        tiles = []
        for tile in range(rows // pieces):
            piece = side[pl.ds(tile * pieces, depth, stride=rows), :]
            for q in range(1, pieces):
                piece = jnp.where(groups[q], side[pl.ds(tile * pieces + q, depth, stride=rows), :], piece)
            tiles.append(piece)
        out_ref[index, :depth] = jnp.concatenate(tiles, axis=1).astype(BF16)
        for tile in range(depth // pieces):
            piece = values[tile * pieces, :, LANES:]
            for q in range(1, pieces):
                piece = jnp.where(groups[q], values[tile * pieces + q, :, LANES:], piece)
            rights[index, :, LANES * tile : LANES * tile + LANES] = piece
        return carry

    lax.fori_loop(0, count, step, 0, unroll=False)
    flat = rights[...].reshape(count * rows, depth * inner).astype(BF16)
    spread = dot(flat, w_spread[...]).reshape(count, rows, depth * inner)
    parts = out_ref.shape[-1]
    for part in range(depth * inner // parts):
        out_ref[:, depth + part * rows : depth + part * rows + rows] = spread[
            :, :, part * parts : part * parts + parts
        ].astype(BF16)
    if send:
        pair_copy.wait()


def project(send, place, lengths, alignment, pair, w_align, w_spread):
    slots, depth, rows, width = alignment.shape
    count = slots // 2
    inner = w_align.shape[1] // 2
    smem = pl.BlockSpec(memory_space=pltpu.SMEM)
    vmem = pl.BlockSpec(memory_space=pltpu.VMEM)
    anywhere = pl.BlockSpec(memory_space=pl.ANY)
    out = jax.ShapeDtypeStruct((count, 2 * depth, rows * inner), BF16)
    pair_out = jax.ShapeDtypeStruct((count,) + pair.shape[1:], BF16)
    return pl.pallas_call(
        functools.partial(project_kernel, send),
        out_shape=(out, pair_out) if send else out,
        in_specs=[smem, smem, anywhere] + [anywhere] * send + [vmem, vmem],
        out_specs=(vmem, vmem) if send else vmem,
        scratch_shapes=[
            pltpu.VMEM((count, depth, rows, width), BF16),
            pltpu.VMEM((depth * rows, LANES), F32),
            pltpu.VMEM((count, rows, depth * inner), F32),
            pltpu.SemaphoreType.DMA((2,)),
        ],
        cost_estimate=pl.CostEstimate(flops=10**9, bytes_accessed=2 * 10**6, transcendentals=0),
        name="project_send" if send else "project_own",
    )(*((place, lengths, alignment) + ((pair,) if send else ()) + (w_align, w_spread)))


def update_kernel(
    place_ref,
    lengths_ref,
    breaks_ref,
    own_sides,
    other_sides,
    pair,
    other_pair,
    w_outer,
    bias,
    out_ab,
    out_gate,
    out_proj,
    in_ab,
    in_gate,
    in_proj,
    keep_ref,
    send_ref,
    own_pair,
    stacked,
    outer,
    updates,
    first,
    second,
    sem,
):
    count, rows, full, width = own_pair.shape
    depth = own_sides.shape[1] // 2
    inner = own_sides.shape[2] // rows
    pieces = LANES // inner
    sets = inner // pieces
    hidden = out_proj.shape[0]
    half = place_ref[0]
    start = place_ref[2]
    home = place_ref[3] + start
    copy = pltpu.make_async_copy(pair.at[pl.ds(start, count)], own_pair, sem.at[0])
    copy.start()
    low_is_own = half == 0
    groups = lane_groups(inner)
    zero = jnp.zeros((), BF16)
    stacked[...] = jnp.zeros_like(stacked)
    place_j = lax.broadcasted_iota(jnp.int32, (full, 1), 0)

    def outer_update(step):
        own, other = own_sides[step], other_sides[step]
        low = jnp.where(low_is_own, own, other)
        high = jnp.where(low_is_own, other, own)
        for tile in range(full // pieces):
            source = low if tile < rows // pieces else high
            at = tile % (rows // pieces) * LANES
            left = source[:depth, at : at + LANES]
            turned = [left] + [pltpu.roll(left, inner * turn, 1) for turn in range(1, pieces)]
            for p in range(pieces):
                column = (tile * pieces + p) * LANES
                for q in range(pieces):
                    stacked[depth * q : depth * q + depth, column : column + LANES] = jnp.where(
                        groups[q], turned[(q - p) % pieces], zero
                    )
        lanes = own_sides.shape[2]
        right = jnp.concatenate(
            [
                jnp.concatenate([low[depth + rows * part : depth + rows * part + rows] for part in range(depth // rows)], axis=1),
                jnp.concatenate([high[depth + rows * part : depth + rows * part + rows] for part in range(depth // rows)], axis=1),
            ],
            axis=0,
        )
        per = LANES // (pieces * depth)
        tiles = []
        for c2 in range(sets):
            tile = right[:, c2 // per * LANES : c2 // per * LANES + LANES]
            turn = c2 % per * pieces * depth
            tiles.append(pltpu.roll(tile, LANES - turn, 1) if turn else tile)
        right = jnp.concatenate(tiles, axis=0)
        for i in range(0, full, 2):
            product = dot(right, stacked[:, LANES * i : LANES * i + 2 * LANES]).astype(BF16)
            for k in range(2):
                for g in range(sets):
                    outer[full * (i + k) : full * (i + k) + full, LANES * g : LANES * g + LANES] = product[
                        full * g : full * g + full, LANES * k : LANES * k + LANES
                    ]
        updates[...] = dot(outer[...], w_outer[...])

    def finish(step):
        length = lengths_ref[home + step]
        stop = breaks_ref[home + step]
        own, other = own_pair[step], other_pair[step]
        low = jnp.where(low_is_own, own, other).reshape(rows * full, width)
        high = jnp.where(low_is_own, other, own).reshape(rows * full, width)
        within, across = bias[0:1].astype(F32), bias[1:2].astype(F32)
        head = place_j < stop
        terms = (jnp.where(head, within, across), jnp.where(head, across, within))
        chain = jnp.concatenate([jnp.where(i < stop, terms[0], terms[1]) for i in range(full)], axis=0)
        column = jnp.where(place_j < length, 1.0, 0.0)
        inside = jnp.concatenate([jnp.where(i < length, column, 0.0) for i in range(full)], axis=0)
        z1 = jnp.concatenate([low, high], axis=0).astype(F32) + updates[...] + chain
        unit = 0.5 * width**0.5
        within_unit = inside * unit

        def sides(values, w_ab, w_gate):
            x = normalize(values, within_unit)
            projected = dot(x, w_ab[...])
            a = (jnp.tanh(projected[:, hidden : 2 * hidden]) + 1.0) * projected[:, :hidden]
            b = (jnp.tanh(projected[:, 3 * hidden :]) + 1.0) * projected[:, 2 * hidden : 3 * hidden]
            gate = jnp.tanh(dot(x, w_gate[...])) + 1.0
            return a, b, gate

        def contract(row_of, columns):
            parts = []
            for i in range(full):
                terms = [row_of(i, k) * columns[k] for k in range(full)]
                while len(terms) > 1:
                    terms = [terms[n] + terms[n + 1] for n in range(0, len(terms), 2)]
                parts.append(terms[0])
            return jnp.concatenate(parts, axis=0)

        a, b, gate = sides(z1, out_ab, out_gate)
        first[...] = a
        second[...] = b
        columns = [second[pl.ds(k, full, stride=full), :] for k in range(full)]
        t = contract(lambda i, k: first[pl.ds(full * i + k, 1), :], columns)
        z2 = (z1 + gate * dot(normalize(t, unit), out_proj[...])).astype(BF16).astype(F32)
        a, b, gate = sides(z2, in_ab, in_gate)
        second[...] = b
        columns = [a[full * k : full * k + full] for k in range(full)]
        t = contract(lambda i, k: second[pl.ds(full * k + i, 1), :], columns)
        y3 = ((z2 + gate * dot(normalize(t, unit), in_proj[...])) * inside).astype(BF16)
        low = y3[: rows * full].reshape(rows, full, width)
        high = y3[rows * full :].reshape(rows, full, width)
        keep_ref[step] = jnp.where(low_is_own, low, high)
        send_ref[step] = jnp.where(low_is_own, high, low)

    outer_update(0)
    copy.wait()

    def both(step, carry):
        finish(step)
        outer_update(jnp.minimum(step + 1, count - 1))
        return carry

    lax.fori_loop(0, count, both, 0)


def update(place, lengths, breaks, own_sides, other_sides, pair, other_pair, weights):
    outer_proj, chain_bias, out_ab, out_gate, out_proj, in_ab, in_gate, in_proj = weights
    count, rows, full, width = other_pair.shape
    depth = own_sides.shape[1] // 2
    inner = own_sides.shape[2] // rows
    smem = pl.BlockSpec(memory_space=pltpu.SMEM)
    vmem = pl.BlockSpec(memory_space=pltpu.VMEM)
    anywhere = pl.BlockSpec(memory_space=pl.ANY)
    shape = jax.ShapeDtypeStruct(other_pair.shape, BF16)
    pairs = full * full
    return pl.pallas_call(
        update_kernel,
        out_shape=(shape, shape),
        in_specs=[smem] * 3 + [vmem] * 2 + [anywhere] + [vmem] * 9,
        out_specs=(vmem, vmem),
        scratch_shapes=[
            pltpu.VMEM(other_pair.shape, BF16),
            pltpu.VMEM((LANES, full * LANES), BF16),
            pltpu.VMEM((pairs, inner * inner), BF16),
            pltpu.VMEM((pairs, width), F32),
            pltpu.VMEM((pairs, width), F32),
            pltpu.VMEM((pairs, width), F32),
            pltpu.SemaphoreType.DMA((1,)),
        ],
        name="pair_update",
    )(
        place,
        lengths,
        breaks,
        own_sides,
        other_sides,
        pair,
        other_pair,
        outer_proj,
        chain_bias,
        out_ab,
        out_gate,
        out_proj,
        in_ab,
        in_gate,
        in_proj,
    )


def spread_matrix(depth, inner):
    pieces = LANES // inner
    r, c2 = np.divmod(np.arange(depth * inner), inner)
    matrix = np.zeros((depth * inner, depth * inner), np.float32)
    matrix[np.arange(depth * inner), (c2 // pieces) * pieces * depth + (c2 % pieces) * depth + r] = 1.0
    return jnp.asarray(matrix, BF16)


def pack_slots(blocks, positions, buffer_slots):
    slot_index = jnp.arange(positions.shape[0], dtype=jnp.int32)
    matches = positions[None, :] == jnp.arange(buffer_slots, dtype=jnp.int32)[:, None]
    source = jnp.sum(jnp.where(matches, slot_index[None, :], 0), axis=1)
    return jnp.take(blocks, source, axis=0)


def body(pair_rep, alignment, lengths, chain_breaks, shifts, *weights):
    group_count = lax.axis_size("pool")
    my_group = lax.axis_index("pool")
    half = lax.axis_index("dap")
    slot_count = pair_rep.shape[0]
    count = slot_count // 2
    capacity = max(2, (2 * slot_count + group_count - 1) // group_count)
    buffer_slots = group_count * capacity
    swap = [(0, 1), (1, 0)]
    mine = half * count
    theirs = (1 - half) * count
    home = my_group * slot_count
    place = jnp.stack([half, theirs, mine, home]).astype(jnp.int32)
    alignment_proj, outer_proj = weights[:2]
    inner = alignment_proj.shape[1] // 2
    w_spread = spread_matrix(alignment.shape[1], inner)
    w_outer = (
        outer_proj.reshape(inner, inner, -1).transpose(1, 0, 2).reshape(outer_proj.shape)
    )
    send_sides, send_pair = project(True, place, lengths, alignment, pair_rep, alignment_proj, w_spread)
    other_sides = lax.ppermute(send_sides, "dap", swap)
    other_pair = lax.ppermute(send_pair, "dap", swap)
    own_sides = project(False, place, lengths, alignment, pair_rep, alignment_proj, w_spread)
    keep, send = update(
        place, lengths, chain_breaks, own_sides, other_sides, pair_rep, other_pair, (w_outer,) + weights[2:]
    )
    received = lax.ppermute(send, "dap", swap)
    result = jnp.concatenate([keep, received], axis=0)

    slot_index = jnp.arange(slot_count, dtype=jnp.int32)
    earlier = (shifts[None, :] == shifts[:, None]) & (slot_index[None, :] < slot_index[:, None])
    slot_rank = jnp.sum(earlier.astype(jnp.int32), axis=1)
    send_at = (my_group + shifts) % group_count * capacity + slot_rank
    send_at = jnp.where(half == 0, send_at, jnp.roll(send_at, count))
    receive_position = (my_group - shifts) % group_count * capacity + slot_rank
    outgoing = pack_slots(result, send_at, buffer_slots)
    received_blocks = lax.all_to_all(outgoing, "pool", split_axis=0, concat_axis=0, tiled=True)
    return jnp.take(received_blocks, receive_position, axis=0)


def solution(mesh):
    return jax.shard_map(
        body,
        mesh=mesh,
        in_specs=(
            P(("screen", "pool"), "dap", None, None),
            P(("screen", "pool"), None, "dap", None),
            P("screen"),
            P("screen"),
            P("screen"),
        )
        + (P(),) * 9,
        out_specs=P(("screen", "pool"), "dap", None, None),
        check_vma=False,
    )
```

time: 92.4 us -> 95.6 us (1.035)
  Pallas kernels: 29.8 us -> 38.9 us
  local copies, waits for them, and re-layouts: 9.01 us -> 4.68 us
  other arithmetic: 6.15 us -> 4.4 us
    pallas_call x0 -> x2, Pallas kernels: none -> 13.6 us  [project(): pl.pallas_call(functools.partial(project_kernel, send), out_shape=(out, p...]
    dynamic_slice x4 -> x0, local copies, waits for them, and re-layouts: 4.49 us -> none  [the longest x1 2.37 us: body(): lax.dynamic_slice_in_dim(alignment, theirs, count)]
    pallas_call x1, Pallas kernels: 29.8 us -> 25.3 us  [update(): pl.pallas_call(update_kernel, out_shape=(shape, shape), in_specs=[smem] *...]
    convert_element_type x1 -> x0, other arithmetic: 1.54 us -> none  [update(): (target == c2 // pieces * 128 + c2 % pieces * depth + r).astype(BF16)]
    unnamed x25 -> x9, local copies, waits for them, and re-layouts: 1.16 us -> 2.27 us
  transfers between devices with their start and end apart: 4 -> 4, of which waited for: 2 -> 2; matrix products, arithmetic and copies ran while one was open for 7% -> 1% of each run, Pallas kernels for 0% -> 7%
where the time goes in v2:
time: 95.6 us; the launch traced here: 95.2 us
  Pallas kernels  38.9 us (41%)
  waiting for transfers between devices  38.8 us (41%)
  starting transfers between devices  8.33 us (9%)
  local copies, waits for them, and re-layouts  4.68 us (5%)
  other arithmetic  4.4 us (5%)
    all_to_all x1, waiting for transfers between devices, body(): lax.all_to_all(outgoing, 'pool', split_axis=0, concat_axis=0, tiled=True)  37.3 us
    pallas_call x1, Pallas kernels, update(): pl.pallas_call(update_kernel, out_shape=(shape, shape), in_specs=[smem] *...  25.3 us
    pallas_call x2, Pallas kernels, project(): pl.pallas_call(functools.partial(project_kernel, send), out_shape=(out, p...  13.6 us
    all_to_all x1, starting transfers between devices, body(): lax.all_to_all(outgoing, 'pool', split_axis=0, concat_axis=0, tiled=True)  7.2 us
    unnamed x9, local copies, waits for them, and re-layouts  2.27 us
  transfers between devices with their start and end apart: 4, of which 2 were waited for; matrix products, arithmetic and copies ran while one was open for 1% of the time, Pallas kernels for 7%

profile of v2, /device:TPU:0, one launch (start us, length us, event | category | flops | bytes accessed | tf_op | source)
XLA Modules:
  0.0 95.2 jit_solution(1981163843952723841)
XLA Ops:
  0.0 1.5 %copy.19.refs_1_.refs_2_ = bf16[256,64]{1,0:T(8,128)(2,1)} copy(bf16[256,64]{0,1:T(8,128)(2,1)} %param.20) | data formatting | bytes 65536 | tf_op args[5]
  1.5 0.6 pad_add_fusion.place_ref
  2.1 6.9 %project_send.1 = (bf16[11,32,256]{2,1,0:T(8,128)(2,1)}, bf16[11,8,16,128]{3,2,1,0:T(8,128)(2,1)}) custom-call(s32[4]{0:T(128)} %pad_add_fusion.place_ref, s32[176]{0:T(256)} %lengths_ref.5, bf16[22,16,8,256]{3,2,1,0:T(8,128)(2,1)} %refs_0_.3, bf16[22,8,16,128]{3,2,1,0:T(8,128)(2,1)} %pair.1, bf16[256,64]{1,0:T(8,128)(2,1)} %copy.19.refs_1_.refs_2_, ...), custom_call_target="tpu_custom_call" | custom-call | flops 1000000000 | bytes 2000000 | tf_op jit(solution)/shard_map/project_send/pallas_call | solution.py:99
  9.0 0.6 collective-permute-start.1
  9.5 0.1 collective-permute-start
  9.6 0.8 copy.21
  10.4 0.2 convert_reduce_fusion
  10.6 0.1 fusion.8
  10.7 0.1 broadcast_select_fusion.2
  10.8 6.7 %project_own.1.own_sides = bf16[11,32,256]{2,1,0:T(8,128)(2,1)} custom-call(s32[4]{0:T(128)} %pad_add_fusion.place_ref, s32[176]{0:T(256)} %lengths_ref.5, bf16[22,16,8,256]{3,2,1,0:T(8,128)(2,1)} %refs_0_.3, bf16[256,64]{1,0:T(8,128)(2,1)} %copy.19.refs_1_.refs_2_, bf16[512,512]{1,0:T(8,128)(2,1)} %constant.67.clone.refs_2_.refs_3_), custom_call_target="tpu_custom_call" | custom-call | flops 1000000000 | bytes 2000000 | tf_op jit(solution)/shard_map/project_own/pallas_call | solution.py:99
  17.5 0.1 select_reduce_fusion
  17.6 0.0 copy-start
  17.6 0.6 copy-done.2
  18.3 0.1 copy-done
  18.4 25.3 %pair_update.1 = (bf16[11,8,16,128]{3,2,1,0:T(8,128)(2,1)}, bf16[11,8,16,128]{3,2,1,0:T(8,128)(2,1)}) custom-call(s32[4]{0:T(128)} %pad_add_fusion.place_ref, s32[176]{0:T(256)} %lengths_ref.5, s32[176]{0:T(256)} %breaks_ref.1, bf16[11,32,256]{2,1,0:T(8,128)(2,1)} %project_own.1.own_sides, bf16[11,32,256]{2,1,0:T(8,128)(2,1)} %copy-done.2, ...), custom_call_target="tpu_custom_call" | custom-call | tf_op jit(solution)/shard_map/pair_update/pallas_call | solution.py:267
  43.7 0.5 collective-permute-start.2
  44.2 1.5 %collective-permute-done.2 = bf16[11,8,16,128]{3,2,1,0:T(8,128)(2,1)S(1)} collective-permute-done((bf16[11,8,16,128]{3,2,1,0:T(8,128)(2,1)}, bf16[11,8,16,128]{3,2,1,0:T(8,128)(2,1)S(1)}, u32[]{:S(2)}, u32[]{:S(2)}) %collective-permute-start.2) | collective-permute-done | bytes 360480 | tf_op jit(solution)/shard_map/ppermute | solution.py:342
  45.7 1.0 %pad_maximum_fusion = bf16[22,8,16,128]{3,2,1,0:T(8,128)(2,1)S(1)} fusion(bf16[11,8,16,128]{3,2,1,0:T(8,128)(2,1)S(1)} %collective-permute-done.2, bf16[11,8,16,128]{3,2,1,0:T(8,128)(2,1)} %get-tuple-element.11), kind=kLoop, calls=%fused_computation.3 | loop fusion | flops 360448 | bytes 1441792 | tf_op jit(solution)/shard_map/concatenate | solution.py:343
  46.8 0.8 gather_fusion
  47.6 1.4 %broadcast_select_fusion = bf16[48,8,16,128]{3,2,1,0:T(8,128)(2,1)} fusion(bf16[48,8,16,128]{3,2,1,0:T(8,128)(2,1)S(1)} %gather_fusion, pred[48]{0:T(512)(128)(4,1)S(1)} %compare_and_fusion), kind=kLoop, calls=%fused_computation.2 | loop fusion | flops 786432 | bytes 3145776 | tf_op jit(solution)/shard_map/jit(_take)/select_n | solution.py:313
  49.0 7.2 %all-to-all-start = ((bf16[48,8,16,128]{3,2,1,0:T(8,128)(2,1)}), bf16[48,8,16,128]{3,2,1,0:T(8,128)(2,1)S(1)}, u32[]{:S(2)}, u32[]{:S(2)}) async-start(bf16[48,8,16,128]{3,2,1,0:T(8,128)(2,1)} %broadcast_select_fusion), calls=%async_computation | async-start | bytes 3145728 | tf_op jit(solution)/shard_map/all_to_all | solution.py:352
  56.2 37.3 %all-to-all-done = bf16[48,8,16,128]{3,2,1,0:T(8,128)(2,1)S(1)} async-done(((bf16[48,8,16,128]{3,2,1,0:T(8,128)(2,1)}), bf16[48,8,16,128]{3,2,1,0:T(8,128)(2,1)S(1)}, u32[]{:S(2)}, u32[]{:S(2)}) %all-to-all-start) | async-done | bytes 1572896 | tf_op jit(solution)/shard_map/all_to_all | solution.py:352
  93.5 0.7 gather_fusion.1
  94.2 1.0 %broadcast_select_fusion.1 = bf16[22,8,16,128]{3,2,1,0:T(8,128)(2,1)} fusion(bf16[22,8,16,128]{3,2,1,0:T(8,128)(2,1)S(1)} %gather_fusion.1, pred[22]{0:T(512)(128)(4,1)S(1)} %get-tuple-element.13), kind=kLoop, calls=%fused_computation.4 | loop fusion | flops 360448 | bytes 1441814 | tf_op jit(solution)/shard_map/jit(_take)/select_n | solution.py:353
  (13 shorter events, 0.1 us)
Async XLA Ops:
  2.1 7.5 %copy-start.1 = (bf16[1024,128]{1,0:T(8,128)(2,1)S(1)}, bf16[1024,128]{1,0:T(8,128)(2,1)}, u32[]{:S(2)}) copy-start(bf16[1024,128]{1,0:T(8,128)(2,1)} %param.21) | copy-start | bytes 786436
  2.1 8.3 %copy-start.3 = (s32[22]{0:T(128)S(1)}, s32[22]{0:T(128)}, u32[]{:S(2)}) copy-start(s32[22]{0:T(128)} %param.19) | copy-start | bytes 268
  9.0 8.6 %collective-permute-start.1 = (bf16[11,8,16,128]{3,2,1,0:T(8,128)(2,1)}, bf16[11,8,16,128]{3,2,1,0:T(8,128)(2,1)S(1)}, u32[]{:S(2)}, u32[]{:S(2)}) collective-permute-start(bf16[11,8,16,128]{3,2,1,0:T(8,128)(2,1)} %get-tuple-element.10), channel_id=1, source_target_pairs={{0,1},{1,0},{2,3},{3,2},{4,5},{5,4},{6,7},{7,6},{8,9},{9,8},{10,11... | collective-permute-start | bytes 1081352 | tf_op jit(solution)/shard_map/ppermute | solution.py:337
  9.5 8.0 %collective-permute-start = (bf16[11,32,256]{2,1,0:T(8,128)(2,1)}, bf16[11,32,256]{2,1,0:T(8,128)(2,1)S(1)}, u32[]{:S(2)}, u32[]{:S(2)}) collective-permute-start(bf16[11,32,256]{2,1,0:T(8,128)(2,1)} %get-tuple-element.9), channel_id=1, source_target_pairs={{0,1},{1,0},{2,3},{3,2},{4,5},{5,4},{6,7},{7,6},{8,9},{9,8},{10,11... | collective-permute-start | bytes 540680 | tf_op jit(solution)/shard_map/ppermute | solution.py:336
  17.6 0.7 copy-start.2
  17.6 0.8 copy-start
  43.7 2.0 %collective-permute-start.2 = (bf16[11,8,16,128]{3,2,1,0:T(8,128)(2,1)}, bf16[11,8,16,128]{3,2,1,0:T(8,128)(2,1)S(1)}, u32[]{:S(2)}, u32[]{:S(2)}) collective-permute-start(bf16[11,8,16,128]{3,2,1,0:T(8,128)(2,1)} %get-tuple-element.12), channel_id=1, source_target_pairs={{0,1},{1,0},{2,3},{3,2},{4,5},{5,4},{6,7},{7,6},{8,9},{9,8},{10,11... | collective-permute-start | bytes 1081352 | tf_op jit(solution)/shard_map/ppermute | solution.py:342
  49.0 44.5 %all-to-all-start = ((bf16[48,8,16,128]{3,2,1,0:T(8,128)(2,1)}), bf16[48,8,16,128]{3,2,1,0:T(8,128)(2,1)S(1)}, u32[]{:S(2)}, u32[]{:S(2)}) async-start(bf16[48,8,16,128]{3,2,1,0:T(8,128)(2,1)} %broadcast_select_fusion), calls=%async_computation | async-start | bytes 3145728 | tf_op jit(solution)/shard_map/all_to_all | solution.py:352
